TPU v7x, 32 devices: a whole 2x2x4 slice. The times are simulated.
32 devices in a mesh: blk: 4 (over y, x), rep: 8 (over z, core).
Axes of the slice: x: 2, y: 2, z: 4, core: 2. Of those that a mesh axis runs over, the one named last changes fastest.
Arguments:
- query_hidden: bfloat16 [8, 16, 32, 768], P('rep', 'blk'), may hold values from -18 to 18
- passage_hidden: bfloat16 [8, 16, 512, 768], P('rep', 'blk'), may hold values from -6 to 6
- lengths: int32 [8, 16], P('rep', 'blk'), may hold values from 64 to 512
- projection: bfloat16 [768, 128], replicated, may hold values from -0.21875 to 0.21875
Outputs:
- query_grad: float32 [8, 16, 32, 128], P('rep', 'blk')
- passage_grad: float32 [8, 16, 512, 128], P('rep', 'blk')
- grad_weight: float32 [768, 128], replicated
- loss: float32 [], replicated
All inputs are finite; a program needn't handle non-finite values.
Results may differ from a plain program's by a relative error of at most 0.0097.
Values may be sent and summed in bfloat16 or wider, within the bound.
A program may use at most 128 MiB of HBM per device.

v0:
```python
import functools

import jax
import jax.numpy as jnp
from jax import lax
from jax.experimental import pallas as pl
from jax.experimental.pallas import tpu as pltpu
from jax.sharding import PartitionSpec as P

MESH = pl.DeviceIdType.MESH
F32 = jnp.float32
BF16 = jnp.bfloat16
NT = (((1,), (1,)), ((), ()))

temper = 0.5


def rows_iota(shape, dim):
    return lax.broadcasted_iota(jnp.int32, shape, dim)


def exact_dot(x, ones):
    high = x.astype(BF16)
    rest = x - high.astype(F32)
    mid = rest.astype(BF16)
    low = (rest - mid.astype(F32)).astype(BF16)
    dot = lambda y: jnp.dot(y, ones, preferred_element_type=F32)
    return dot(high) + (dot(mid) + dot(low))


def kernel(
    dims, lens_in, qhid_in, proj_in, phid, qg_out, pg_v, cbuf, loss_out,
    lens, qhid, proj, pick, spread, tok, ptok, ptok_t, phid_v, expo, grad_a, sums, pooled, sc, lo, qsend, qrecv,
    wsend, wrecv, zbuf,
    in_sem, tok_s, tok_r, sc_s, sc_r, lo_s, lo_r, qg_s, qg_r, ws_s, ws_r, z_s, z_r, c_s, c_r,
):
    nblk, nrep, ncore, nquery, qlen, npass, plen = dims
    ntok = nquery * qlen
    nqi = nblk * ntok
    nq_all = nblk * nquery
    nz = nrep // ncore
    na = nblk * ncore
    dim = proj.shape[1]
    total = nq_all * nrep
    blk = lax.axis_index("blk")
    rep = lax.axis_index("rep")
    core = lax.rem(rep, ncore)
    zed = rep // ncore
    me_a = blk * ncore + core

    def blk_peer(k):
        return (lax.rem(blk + k, nblk), rep)

    def rep_peer(k):
        return (blk, lax.rem(rep + k, nrep))

    def a_index(k):
        return lax.rem(me_a + k, na)

    def a_peer(k):
        other = a_index(k)
        return (other // ncore, zed * ncore + lax.rem(other, ncore))

    def z_peer(k):
        return (blk, lax.rem(zed + k, nz) * ncore + core)

    def share(src, dst, send, recv, peer, count):
        copies = []
        for k in range(1, count):
            copy = pltpu.make_async_remote_copy(
                src_ref=src(k), dst_ref=dst, send_sem=send.at[k - 1], recv_sem=recv.at[k - 1],
                device_id=peer(k), device_id_type=MESH,
            )
            copy.start()
            copies.append(copy)
        return copies

    barrier = pltpu.get_barrier_semaphore()
    greeted = 0
    for count, peer in ((na, a_peer), (nrep, rep_peer)):
        for k in range(1, count):
            pl.semaphore_signal(barrier, inc=1, device_id=peer(k), device_id_type=MESH)
            greeted += 1

    loads = []
    pairs = [(qhid_in, qhid), (proj_in, proj), (lens_in, lens)]
    pairs += [(phid.at[p], phid_v.at[p]) for p in range(npass)]
    for n, (src, dst) in enumerate(pairs):
        load = pltpu.make_async_copy(src, dst, in_sem.at[n])
        load.start()
        loads.append(load)
    qpad = sc.shape[2]
    owner = rows_iota((nqi, qpad), 1) * qlen
    token = rows_iota((nqi, qpad), 0)
    pick[...] = jnp.where((token >= owner) & (token < owner + qlen), 1.0, 0.0).astype(BF16)
    owner_t = rows_iota((qpad, nqi), 0) * qlen
    token_t = rows_iota((qpad, nqi), 1)
    spread[...] = jnp.where((token_t >= owner_t) & (token_t < owner_t + qlen), 1.0, 0.0).astype(BF16)
    pooled[...] = jnp.zeros_like(pooled)
    sums[...] = jnp.ones_like(sums)
    loads[0].wait()
    loads[1].wait()
    tok[blk] = jnp.dot(qhid[...], proj[...], preferred_element_type=F32).astype(BF16)
    pl.semaphore_wait(barrier, greeted)
    tok_copies = share(lambda k: tok.at[blk], tok.at[blk], tok_s, tok_r, blk_peer, nblk)

    loads[2].wait()
    for p in range(npass):
        loads[3 + p].wait()
        vec = jnp.dot(phid_v[p], proj[...], preferred_element_type=F32).astype(BF16)
        ptok[p] = vec
        ptok_t[p] = vec.T
    for copy in tok_copies:
        copy.wait_recv()
    every = tok[...].reshape(nqi, dim)

    def forward(p, carry):
        count = lens[0, p]
        a = lax.dot_general(ptok[p], every, NT, preferred_element_type=F32)
        valid = rows_iota(a.shape, 0) < count
        scaled = jnp.where(valid, a / temper, -jnp.inf)
        top = jnp.max(scaled, 0, keepdims=True)
        e = jnp.exp(scaled - top)
        expo[p] = e
        s = jnp.sum(e, 0, keepdims=True)
        sums[pl.ds(p, 1), :] = s
        size = jnp.log(jnp.full((1, nqi), count, jnp.int32).astype(F32))
        pooled[pl.ds(p, 1), :] = temper * (top + jnp.log(s) - size)
        return carry

    lax.fori_loop(0, npass, forward, 0)

    own = exact_dot(pooled[...], pick[...])
    sc[blk] = own
    sc_copies = share(lambda k: sc.at[blk], sc.at[blk], sc_s, sc_r, blk_peer, nblk)
    inv = 1.0 / sums[...]
    for copy in sc_copies:
        copy.wait_recv()

    score = sc[...]
    row = rows_iota(score.shape, 1)
    lane = rows_iota(score.shape, 2)
    slot = rows_iota(score.shape, 0)
    live = row < npass
    hidden_score = jnp.where(live, score, -jnp.inf)
    top = jnp.max(jnp.max(hidden_score, 0), 0, keepdims=True)
    lse = top + jnp.log(jnp.sum(jnp.sum(jnp.exp(hidden_score - top[None]), 0), 0, keepdims=True))
    mine = rows_iota(own.shape, 0) + blk * npass == rows_iota(own.shape, 1)
    dscore = (jnp.exp(own - lse) - mine.astype(F32)) / total
    factor = exact_dot(dscore, spread[...]) * inv
    sums[...] = factor

    def backward(p, acc):
        d = (expo[p] * sums[pl.ds(p, 1), :]).astype(BF16)
        grad_a[p] = d
        return acc + jnp.dot(ptok_t[p], d, preferred_element_type=F32)

    qg_t = lax.fori_loop(0, npass, backward, jnp.zeros((dim, nqi), F32))
    for b in range(nblk):
        qsend[b] = qg_t[:, b * ntok : (b + 1) * ntok].astype(BF16)
    qrecv[blk] = qsend[blk]
    qg_copies = share(lambda k: qsend.at[lax.rem(blk + k, nblk)], qrecv.at[blk], qg_s, qg_r, blk_peer, nblk)

    hit = live & (slot * npass + row == lane)
    aim = jnp.sum(jnp.sum(jnp.where(hit, score, 0.0), 0), 0, keepdims=True)
    gap = jnp.where(rows_iota(lse.shape, 1) < nq_all, lse - aim, 0.0)
    part = jnp.sum(gap, 1, keepdims=True)
    lo[rep] = jnp.broadcast_to(part, lo.shape[1:])
    lo_copies = share(lambda k: lo.at[rep], lo.at[rep], lo_s, lo_r, rep_peer, nrep)


    def passages(p, acc):
        g = jnp.dot(grad_a[p], every, preferred_element_type=F32)
        pg_v[p] = g
        return acc + jnp.dot(g.astype(BF16).T, phid_v[p], preferred_element_type=F32)

    wg_t = lax.fori_loop(0, npass, passages, jnp.zeros((dim, qhid.shape[1]), F32))
    for copy in qg_copies:
        copy.wait_recv()
    mine_t = jnp.sum(qrecv[...].astype(F32), 0)
    wg_t = wg_t + jnp.dot(mine_t.astype(BF16), qhid[...], preferred_element_type=F32)
    depth = dim // na
    for a in range(na):
        wsend[a] = wg_t[a * depth : (a + 1) * depth].astype(BF16)
    wrecv[me_a] = wsend[me_a]
    ws_copies = share(lambda k: wsend.at[a_index(k)], wrecv.at[me_a], ws_s, ws_r, a_peer, na)
    qg_out[...] = mine_t.T
    for copy in ws_copies:
        copy.wait_recv()
    zbuf[zed] = jnp.sum(wrecv[...].astype(F32), 0).astype(BF16)
    z_copies = share(lambda k: zbuf.at[zed], zbuf.at[zed], z_s, z_r, z_peer, nz)
    for copy in lo_copies:
        copy.wait_recv()
    loss_out[...] = jnp.sum(lo[...], 0) / total
    for copy in z_copies:
        copy.wait_recv()
    cbuf[me_a] = jnp.sum(zbuf[...].astype(F32), 0).astype(BF16)
    c_copies = share(lambda k: cbuf.at[me_a], cbuf.at[me_a], c_s, c_r, a_peer, na)
    for copy in tok_copies + sc_copies + lo_copies + qg_copies + ws_copies + z_copies:
        copy.wait_send()
    for copy in c_copies:
        copy.wait_recv()
    for copy in c_copies:
        copy.wait_send()


def write_out(qg, pg, wg_t, loss, qg_out, pg_out, wg_out, loss_out, wg_v, sem):
    first = pltpu.make_async_copy(pg, pg_out, sem.at[0])
    first.start()
    second = pltpu.make_async_copy(qg, qg_out, sem.at[1])
    second.start()
    na, depth, hidden = wg_t.shape
    wg_v[...] = wg_t[...].astype(F32).reshape(na * depth, hidden).T
    third = pltpu.make_async_copy(wg_v, wg_out, sem.at[2])
    third.start()
    loss_out[0, 0] = loss[0, 0]
    first.wait()
    second.wait()
    third.wait()


def shards(query_hidden, passage_hidden, lengths, projection):
    hidden, dim = projection.shape
    nquery, qlen = query_hidden.shape[1:3]
    npass, plen = passage_hidden.shape[1:3]
    nblk = lax.axis_size("blk")
    nrep = lax.axis_size("rep")
    ncore = 2 if nrep % 2 == 0 else 1
    nz = nrep // ncore
    na = nblk * ncore
    ntok = nquery * qlen
    nqi = nblk * ntok
    ppad = -(-npass // 8) * 8
    qpad = -(-nblk * nquery // 128) * 128
    dims = (nblk, nrep, ncore, nquery, qlen, npass, plen)
    vmem = pl.BlockSpec(memory_space=pltpu.VMEM)
    sem = lambda n: pltpu.SemaphoreType.DMA((max(n, 1),))
    pairs = []
    for n in (nblk, nblk, nrep, nblk, na, nz, na):
        pairs += [sem(n - 1), sem(n - 1)]
    held = pl.pallas_call(
        functools.partial(kernel, dims),
        out_shape=(
            pltpu.VMEM((ntok, dim), F32),
            pltpu.VMEM((npass, plen, dim), F32),
            pltpu.VMEM((na, dim // na, hidden), BF16),
            pltpu.VMEM((8, 128), F32),
        ),
        in_specs=[
            *[pl.BlockSpec(memory_space=pl.ANY)] * 4,
        ],
        out_specs=(vmem, vmem, vmem, vmem),
        scratch_shapes=[
            pltpu.SMEM((1, npass), jnp.int32),
            pltpu.VMEM((ntok, hidden), BF16),
            pltpu.VMEM((hidden, dim), BF16),
            pltpu.VMEM((nqi, qpad), BF16),
            pltpu.VMEM((qpad, nqi), BF16),
            pltpu.VMEM((nblk, ntok, dim), BF16),
            pltpu.VMEM((npass, plen, dim), BF16),
            pltpu.VMEM((npass, dim, plen), BF16),
            pltpu.VMEM((npass, plen, hidden), BF16),
            pltpu.VMEM((npass, plen, nqi), F32),
            pltpu.VMEM((npass, plen, nqi), BF16),
            pltpu.VMEM((ppad, nqi), F32),
            pltpu.VMEM((ppad, nqi), F32),
            pltpu.VMEM((nblk, ppad, qpad), F32),
            pltpu.VMEM((nrep, 8, 128), F32),
            pltpu.VMEM((nblk, dim, ntok), BF16),
            pltpu.VMEM((nblk, dim, ntok), BF16),
            pltpu.VMEM((na, dim // na, hidden), BF16),
            pltpu.VMEM((na, dim // na, hidden), BF16),
            pltpu.VMEM((nz, dim // na, hidden), BF16),
            sem(npass + 3),
        ] + pairs,
        compiler_params=pltpu.CompilerParams(
            collective_id=0, has_side_effects=True, vmem_limit_bytes=56 << 20
        ),
    )(
        lengths,
        query_hidden.reshape(ntok, hidden),
        projection,
        passage_hidden.reshape(npass, plen, hidden),
    )
    hbm = pl.BlockSpec(memory_space=pl.ANY)
    qg, pg, wg, loss = pl.pallas_call(
        write_out,
        out_shape=(
            jax.ShapeDtypeStruct((ntok, dim), F32),
            jax.ShapeDtypeStruct((npass, plen, dim), F32),
            jax.ShapeDtypeStruct((hidden, dim), F32),
            jax.ShapeDtypeStruct((1, 1), F32),
        ),
        in_specs=[vmem] * 4,
        out_specs=(hbm, hbm, hbm, pl.BlockSpec(memory_space=pltpu.SMEM)),
        scratch_shapes=[pltpu.VMEM((hidden, dim), F32), sem(3)],
        compiler_params=pltpu.CompilerParams(vmem_limit_bytes=8 << 20),
    )(*[pltpu.with_memory_space_constraint(x, pltpu.VMEM) for x in held])
    return (
        qg.reshape(1, nquery, qlen, dim),
        pg.reshape(1, npass, plen, dim),
        wg,
        loss.reshape(()),
    )


def solution(mesh):
    return jax.shard_map(
        shards,
        mesh=mesh,
        in_specs=(P("rep", "blk", None, None), P("rep", "blk", None, None), P("rep", "blk"), P()),
        out_specs=(P("rep", "blk", None, None), P("rep", "blk", None, None), P(), P()),
        check_vma=False,
    )
```

profile of v0, /device:TPU:0, one launch (start us, length us, event | category | flops | bytes accessed | tf_op | source)
XLA Modules:
  0.0 33.7 jit_solution(13045647137931959421)
XLA Ops:
  0.6 31.4 %shard_map.75 = (f32[128,128]{1,0:T(8,128)S(1)}, f32[4,512,128]{2,1,0:T(8,128)S(1)}, bf16[8,16,768]{2,1,0:T(8,128)(2,1)S(1)}, f32[8,128]{1,0:T(8,128)S(1)}) custom-call(s32[1,4]{1,0:T(1,128)} %lens_in.1, bf16[128,768]{1,0:T(8,128)(2,1)} %bitcast.6, bf16[768,128]{1,0:T(8,128)(2,1)} %proj_in.1, bf16[4,512,768]{2,1,0:T(8,128)(2,1)} %bitcast.5), custom_call_target="tpu_custom_call" | custom-call | tf_op jit(solution)/shard_map/pallas_call | solution.py:241
  32.0 1.7 %shard_map.76 = (f32[128,128]{1,0:T(8,128)}, f32[4,512,128]{2,1,0:T(8,128)}, f32[768,128]{1,0:T(8,128)}, f32[1,1]{1,0:T(1,128)}) custom-call(f32[128,128]{1,0:T(8,128)S(1)} %get-tuple-element.12.qg, f32[4,512,128]{2,1,0:T(8,128)S(1)} %get-tuple-element.13.pg, bf16[8,16,768]{2,1,0:T(8,128)(2,1)S(1)} %get-tuple-element.14.wg_t, ...), custom_call_target="tpu_custom_call" | custom-call | tf_op jit(solution)/shard_map/pallas_call | solution.py:286
where the time goes:
time: 33.8 us; the launch traced here: 33.7 us
  Pallas kernels  33 us (98%)
  between operations  0.64 us (2%)
    pallas_call x1, Pallas kernels, shards(): pl.pallas_call(functools.partial(kernel, dims), out_shape=(pltpu.VMEM((nt...  31.4 us
    pallas_call x1, Pallas kernels, shards(): pl.pallas_call(write_out, out_shape=(jax.ShapeDtypeStruct((ntok, dim), F3...  1.66 us

commit v1 on v0

v1 whole, which is shorter than its diff:
```python
import functools

import jax
import jax.numpy as jnp
from jax import lax
from jax.experimental import pallas as pl
from jax.experimental.pallas import tpu as pltpu
from jax.sharding import PartitionSpec as P

MESH = pl.DeviceIdType.MESH
F32 = jnp.float32
BF16 = jnp.bfloat16
NT = (((1,), (1,)), ((), ()))

temper = 0.5
LANES = 128
LOG2E = 1.4426950408889634
FAR = -1e30


def rows_iota(shape, dim):
    return lax.broadcasted_iota(jnp.int32, shape, dim)


def split_dot(x, ones, terms):
    out = None
    for _ in range(terms):
        part = x.astype(BF16)
        x = x - part.astype(F32)
        dot = jnp.dot(part, ones, preferred_element_type=F32)
        out = dot if out is None else out + dot
    return out


def kernel(
    dims, lens_in, qhid_in, proj_in, phid, qg_out, pg_v, wg_out, loss_out,
    lens, proj, pick, spread, tok, ptok, ptok_t, hid, expo, reach, grads, tops, sums, sc, lo_c, lo_z, qsend, qrecv,
    wsend, wrecv, zbuf, cbuf,
    in_sem, up, down, tok_s, tok_r, hid_s, hid_r, sc_s, sc_r, lc_s, lc_r, lz_s, lz_r, qg_s, qg_r, ws_s, ws_r,
    z_s, z_r, c_s, c_r,
):
    nblk, nrep, ncore, nquery, qlen, npass, plen = dims
    ntok = nquery * qlen
    nqi = nblk * ntok
    nq_all = nblk * nquery
    ntp = npass * plen
    nz = nrep // ncore
    na = nblk * ncore
    hidden, dim = proj.shape
    total = nq_all * nrep
    parts = wsend.shape[0]
    cols = hidden // parts
    paired = nblk & (nblk - 1) == 0
    blk = lax.axis_index("blk")
    rep = lax.axis_index("rep")
    core = lax.rem(rep, ncore)
    zed = rep // ncore
    me_a = blk * ncore + core

    def blk_at(k):
        if not paired:
            return lax.rem(blk + k, nblk)
        out = 0
        bit = 1
        while bit < nblk:
            out = out + lax.rem(blk // bit + k // bit, 2) * bit
            bit *= 2
        return out

    def slot_owner(slots):
        return slots ^ blk if paired else lax.rem(blk + nblk - slots, nblk)

    def blk_peer(k):
        return (blk_at(k), rep)

    def core_peer(k):
        return (blk, zed * ncore + lax.rem(core + k, ncore))

    def a_index(k):
        return lax.rem(me_a + k, na)

    def a_peer(k):
        other = a_index(k)
        return (other // ncore, zed * ncore + lax.rem(other, ncore))

    def z_peer(k):
        return (blk, lax.rem(zed + k, nz) * ncore + core)

    def z_next(step):
        return (blk, (zed + step) * ncore + core)

    def share(src, dst, send, recv, peer, count):
        copies = []
        for k in range(1, count):
            copy = pltpu.make_async_remote_copy(
                src_ref=src(k), dst_ref=dst(k), send_sem=send.at[k - 1], recv_sem=recv.at[k - 1],
                device_id=peer(k), device_id_type=MESH,
            )
            copy.start()
            copies.append(copy)
        return copies

    def tell(step):
        @pl.when((zed >= step) & (zed + 1 < nz))
        def _():
            pl.semaphore_signal(up.at[step - 1], inc=1, device_id=z_next(1), device_id_type=MESH)

        @pl.when((zed + step < nz) & (zed >= 1))
        def _():
            pl.semaphore_signal(down.at[step - 1], inc=1, device_id=z_next(-1), device_id_type=MESH)

    def hear(step):
        @pl.when(zed >= step + 1)
        def _():
            pl.semaphore_wait(up.at[step - 1], 1)

        @pl.when(zed + step + 1 < nz)
        def _():
            pl.semaphore_wait(down.at[step - 1], 1)

    barrier = pltpu.get_barrier_semaphore()
    for k in range(1, na):
        pl.semaphore_signal(barrier, inc=1, device_id=a_peer(k), device_id_type=MESH)

    @pl.when(zed + 1 < nz)
    def _():
        pl.semaphore_signal(barrier, inc=1, device_id=z_next(1), device_id_type=MESH)

    @pl.when(zed >= 1)
    def _():
        pl.semaphore_signal(barrier, inc=1, device_id=z_next(-1), device_id_type=MESH)

    greeted = na - 1 + (zed + nz - 1) // nz + (2 * nz - 2 - zed) // nz

    loads = []
    pairs = [(qhid_in, hid.at[pl.ds(ntp, ntok)]), (proj_in, proj), (lens_in, lens)]
    pairs += [(phid.at[p], hid.at[pl.ds(p * plen, plen)]) for p in range(npass)]
    for n, (src, dst) in enumerate(pairs):
        load = pltpu.make_async_copy(src, dst, in_sem.at[n])
        load.start()
        loads.append(load)
    ppad, qpad = sc.shape[1:]
    token = rows_iota((nqi, qpad), 0)
    query = slot_owner(token // ntok) * nquery + lax.rem(token, ntok) // qlen
    pick[...] = jnp.where(query == rows_iota((nqi, qpad), 1), 1.0, 0.0).astype(BF16)
    token_t = rows_iota((qpad, nqi), 1)
    query_t = slot_owner(token_t // ntok) * nquery + lax.rem(token_t, ntok) // qlen
    spread[...] = jnp.where(query_t == rows_iota((qpad, nqi), 0), 1.0, 0.0).astype(BF16)
    tops[...] = jnp.zeros_like(tops)
    sums[...] = jnp.ones_like(sums)
    unit = jnp.where(rows_iota((ntok, LANES), 1) == 0, 1.0, 0.0).astype(BF16)
    loads[0].wait()
    loads[1].wait()
    tok[0] = jnp.dot(hid[ntp : ntp + ntok, :], proj[...], preferred_element_type=F32).astype(BF16)
    pl.semaphore_wait(barrier, greeted)
    tok_copies = share(lambda k: tok.at[0], lambda k: tok.at[k], tok_s, tok_r, blk_peer, nblk)
    hid_copies = share(
        lambda k: qhid_in, lambda k: hid.at[pl.ds(ntp + k * ntok, ntok)], hid_s, hid_r, blk_peer, nblk
    )
    if nz > 2:
        tell(1)

    loads[2].wait()
    size = jnp.ones((ppad, LANES), jnp.int32)
    for p in range(npass):
        loads[3 + p].wait()
        vec = jnp.dot(hid[p * plen : (p + 1) * plen, :], proj[...], preferred_element_type=F32).astype(BF16)
        ptok[p, :, :dim] = vec
        out_of = (rows_iota((plen, LANES), 0) >= lens[0, p]) & (rows_iota((plen, LANES), 1) == 0)
        ptok[p, :, dim:] = jnp.where(out_of, FAR, 0.0).astype(BF16)
        ptok_t[p] = vec.T
        size = jnp.where(rows_iota((ppad, LANES), 0) == p, lens[0, p], size)

    def forward(first, count):
        width = count * ntok
        side = jnp.concatenate([tok[k] for k in range(first, first + count)], 0)
        side = jnp.concatenate([side, jnp.concatenate([unit] * count, 0)], 1)
        here = pl.ds(first * ntok, width)
        for p in range(npass):
            a = lax.dot_general(ptok[p], side, NT, preferred_element_type=F32)
            top = jnp.max(a, 0, keepdims=True)
            e = jnp.exp2((a - top) * (LOG2E / temper))
            expo[p, :, here] = e.astype(BF16)
            tops[pl.ds(p, 1), here] = top
            sums[pl.ds(p, 1), here] = jnp.sum(e, 0, keepdims=True)

    forward(0, 1)
    for k in range(1, nblk - 1):
        tok_copies[k - 1].wait_recv()
    if nblk > 2:
        forward(1, nblk - 2)
    if nblk > 1:
        tok_copies[nblk - 2].wait_recv()
        forward(nblk - 1, 1)

    log_size = jnp.log(size.astype(F32))[:, :1]
    pooled = temper * (tops[...] * (1.0 / temper) + jnp.log(sums[...]) - log_size)
    own = split_dot(pooled, pick[...], 3)
    sc[0] = own
    sc_copies = share(lambda k: sc.at[0], lambda k: sc.at[k], sc_s, sc_r, blk_peer, nblk)
    inv = 1.0 / sums[...]
    every_t = jnp.concatenate([tok[k].astype(F32).T for k in range(nblk)], 1)
    for p in range(npass):
        reach[p] = jnp.dot(ptok_t[p], expo[p], preferred_element_type=F32)
    if nz > 2:
        for step in range(1, nz - 1):
            hear(step)
            if step + 1 < nz - 1:
                tell(step + 1)
    for copy in sc_copies:
        copy.wait_recv()

    score = sc[...]
    row = rows_iota(score.shape, 1)
    lane = rows_iota(score.shape, 2)
    slot = rows_iota(score.shape, 0)
    live = row < npass
    hidden_score = jnp.where(live, score, -jnp.inf)
    top = jnp.max(jnp.max(hidden_score, 0), 0, keepdims=True)
    lse = top + jnp.log(jnp.sum(jnp.sum(jnp.exp(hidden_score - top[None]), 0), 0, keepdims=True))
    mine = rows_iota(own.shape, 0) + blk * npass == rows_iota(own.shape, 1)
    dscore = (jnp.exp(sc[0] - lse) - mine.astype(F32)) / total
    factor = split_dot(dscore, spread[...], 3) * inv

    qg_t = reach[0] * factor[0:1]
    for p in range(1, npass):
        qg_t = qg_t + reach[p] * factor[p : p + 1]
    qg_b = qg_t.astype(BF16)
    grads[:, ntp:] = qg_b
    for k in range(1, nblk):
        qsend[k] = qg_b[:, k * ntok : (k + 1) * ntok]
    qg_copies = share(lambda k: qsend.at[k], lambda k: qrecv.at[k], qg_s, qg_r, blk_peer, nblk)

    for p in range(npass):
        side = (every_t * factor[p : p + 1]).astype(BF16)
        g = lax.dot_general(expo[p], side, NT, preferred_element_type=F32)
        pg_v[p] = g
        grads[:, p * plen : (p + 1) * plen] = g.astype(BF16).T

    hit = live & (slot_owner(slot) * npass + row == lane)
    aim = jnp.sum(jnp.sum(jnp.where(hit, score, 0.0), 0), 0, keepdims=True)
    gap = jnp.where(rows_iota(lse.shape, 1) < nq_all, lse - aim, 0.0)
    lo_c[core] = jnp.broadcast_to(jnp.sum(gap, 1, keepdims=True), lo_c.shape[1:])
    lc_copies = share(lambda k: lo_c.at[core], lambda k: lo_c.at[core], lc_s, lc_r, core_peer, ncore)

    for copy in hid_copies:
        copy.wait_recv()
    ws_copies = []
    for h in range(parts):
        w = jnp.dot(grads[...], hid[:, h * cols : (h + 1) * cols], preferred_element_type=F32)
        w = w.T.astype(BF16).reshape(na, cols // na, dim)
        wsend[h] = w
        wrecv[h, me_a] = wsend[h, me_a]
        ws_copies.append(share(
            lambda k: wsend.at[h, a_index(k)], lambda k: wrecv.at[h, me_a], ws_s.at[h], ws_r.at[h], a_peer, na
        ))

    for copy in lc_copies:
        copy.wait_recv()
    lo_z[zed] = jnp.sum(lo_c[...], 0)
    lz_copies = share(lambda k: lo_z.at[zed], lambda k: lo_z.at[zed], lz_s, lz_r, z_peer, nz)
    for copy in qg_copies:
        copy.wait_recv()
    mine_t = grads[:, ntp : ntp + ntok].astype(F32)
    for k in range(1, nblk):
        mine_t = mine_t + qrecv[k].astype(F32)
    qg_out[...] = mine_t.T

    z_copies = []
    for h in range(parts):
        for copy in ws_copies[h]:
            copy.wait_recv()
        zbuf[h, zed] = jnp.sum(wrecv[h].astype(F32), 0).astype(BF16)
        z_copies.append(share(
            lambda k: zbuf.at[h, zed], lambda k: zbuf.at[h, zed], z_s.at[h], z_r.at[h], z_peer, nz
        ))
    for copy in lz_copies:
        copy.wait_recv()
    loss_out[...] = jnp.sum(lo_z[...], 0) / total
    c_copies = []
    for h in range(parts):
        for copy in z_copies[h]:
            copy.wait_recv()
        cbuf[h, me_a] = jnp.sum(zbuf[h].astype(F32), 0).astype(BF16)
        c_copies.append(share(
            lambda k: cbuf.at[h, me_a], lambda k: cbuf.at[h, me_a], c_s.at[h], c_r.at[h], a_peer, na
        ))
    for copy in tok_copies + hid_copies + sc_copies + qg_copies + lc_copies + lz_copies:
        copy.wait_send()
    for h in range(parts):
        for copy in ws_copies[h] + z_copies[h]:
            copy.wait_send()
    for h in range(parts):
        for copy in c_copies[h]:
            copy.wait_recv()
        wg_out[h * cols : (h + 1) * cols, :] = cbuf[h].astype(F32).reshape(cols, dim)
    for h in range(parts):
        for copy in c_copies[h]:
            copy.wait_send()


def write_out(qg, pg, wg, loss, qg_out, pg_out, wg_out, loss_out, sem):
    copies = []
    for n, (src, dst) in enumerate(((pg, pg_out), (wg, wg_out), (qg, qg_out))):
        copy = pltpu.make_async_copy(src, dst, sem.at[n])
        copy.start()
        copies.append(copy)
    loss_out[0, 0] = loss[0, 0]
    for copy in copies:
        copy.wait()


def shards(query_hidden, passage_hidden, lengths, projection):
    hidden, dim = projection.shape
    nquery, qlen = query_hidden.shape[1:3]
    npass, plen = passage_hidden.shape[1:3]
    nblk = lax.axis_size("blk")
    nrep = lax.axis_size("rep")
    ncore = 2 if nrep % 2 == 0 else 1
    nz = nrep // ncore
    na = nblk * ncore
    ntok = nquery * qlen
    nqi = nblk * ntok
    ntp = npass * plen
    ppad = -(-npass // 8) * 8
    qpad = -(-nblk * nquery // LANES) * LANES
    parts = 3 if hidden % (3 * 16 * na) == 0 else 1
    deep = hidden // parts // na
    dims = (nblk, nrep, ncore, nquery, qlen, npass, plen)
    vmem = pl.BlockSpec(memory_space=pltpu.VMEM)
    sem = lambda *n: pltpu.SemaphoreType.DMA(tuple(max(i, 1) for i in n))
    flag = pltpu.SemaphoreType.REGULAR((max(nz - 2, 1),))
    pairs = []
    for n in (nblk, nblk, nblk, ncore, nz, nblk):
        pairs += [sem(n - 1), sem(n - 1)]
    for n in (na, nz, na):
        pairs += [sem(parts, n - 1), sem(parts, n - 1)]
    held = pl.pallas_call(
        functools.partial(kernel, dims),
        out_shape=(
            pltpu.VMEM((ntok, dim), F32),
            pltpu.VMEM((npass, plen, dim), F32),
            pltpu.VMEM((hidden, dim), F32),
            pltpu.VMEM((8, LANES), F32),
        ),
        in_specs=[
            *[pl.BlockSpec(memory_space=pl.ANY)] * 4,
        ],
        out_specs=(vmem, vmem, vmem, vmem),
        scratch_shapes=[
            pltpu.SMEM((1, npass), jnp.int32),
            pltpu.VMEM((hidden, dim), BF16),
            pltpu.VMEM((nqi, qpad), BF16),
            pltpu.VMEM((qpad, nqi), BF16),
            pltpu.VMEM((nblk, ntok, dim), BF16),
            pltpu.VMEM((npass, plen, dim + LANES), BF16),
            pltpu.VMEM((npass, dim, plen), BF16),
            pltpu.VMEM((ntp + nqi, hidden), BF16),
            pltpu.VMEM((npass, plen, nqi), BF16),
            pltpu.VMEM((npass, dim, nqi), F32),
            pltpu.VMEM((dim, ntp + nqi), BF16),
            pltpu.VMEM((ppad, nqi), F32),
            pltpu.VMEM((ppad, nqi), F32),
            pltpu.VMEM((nblk, ppad, qpad), F32),
            pltpu.VMEM((ncore, 8, LANES), F32),
            pltpu.VMEM((nz, 8, LANES), F32),
            pltpu.VMEM((nblk, dim, ntok), BF16),
            pltpu.VMEM((nblk, dim, ntok), BF16),
            pltpu.VMEM((parts, na, deep, dim), BF16),
            pltpu.VMEM((parts, na, deep, dim), BF16),
            pltpu.VMEM((parts, nz, deep, dim), BF16),
            pltpu.VMEM((parts, na, deep, dim), BF16),
            sem(npass + 3),
            flag,
            flag,
        ] + pairs,
        compiler_params=pltpu.CompilerParams(
            collective_id=0, has_side_effects=True, vmem_limit_bytes=56 << 20
        ),
    )(
        lengths,
        query_hidden.reshape(ntok, hidden),
        projection,
        passage_hidden.reshape(npass, plen, hidden),
    )
    hbm = pl.BlockSpec(memory_space=pl.ANY)
    qg, pg, wg, loss = pl.pallas_call(
        write_out,
        out_shape=(
            jax.ShapeDtypeStruct((ntok, dim), F32),
            jax.ShapeDtypeStruct((npass, plen, dim), F32),
            jax.ShapeDtypeStruct((hidden, dim), F32),
            jax.ShapeDtypeStruct((1, 1), F32),
        ),
        in_specs=[vmem] * 4,
        out_specs=(hbm, hbm, hbm, pl.BlockSpec(memory_space=pltpu.SMEM)),
        scratch_shapes=[sem(3)],
        compiler_params=pltpu.CompilerParams(vmem_limit_bytes=8 << 20),
    )(*[pltpu.with_memory_space_constraint(x, pltpu.VMEM) for x in held])
    return (
        qg.reshape(1, nquery, qlen, dim),
        pg.reshape(1, npass, plen, dim),
        wg,
        loss.reshape(()),
    )


def solution(mesh):
    return jax.shard_map(
        shards,
        mesh=mesh,
        in_specs=(P("rep", "blk", None, None), P("rep", "blk", None, None), P("rep", "blk"), P()),
        out_specs=(P("rep", "blk", None, None), P("rep", "blk", None, None), P(), P()),
        check_vma=False,
    )
```

time: 33.8 us -> 34.3 us (1.015)
  Pallas kernels: 33 us -> 33.5 us
    pallas_call x1, Pallas kernels: 31.4 us -> 31.8 us  [shards(): pl.pallas_call(functools.partial(kernel, dims), out_shape=(pltpu.VMEM((nt...]
where the time goes in v1:
time: 34.3 us; the launch traced here: 34.1 us
  Pallas kernels  33.5 us (98%)
  between operations  0.64 us (2%)
    pallas_call x1, Pallas kernels, shards(): pl.pallas_call(functools.partial(kernel, dims), out_shape=(pltpu.VMEM((nt...  31.8 us
    pallas_call x1, Pallas kernels, shards(): pl.pallas_call(write_out, out_shape=(jax.ShapeDtypeStruct((ntok, dim), F3...  1.65 us

profile of v1, /device:TPU:0, one launch (start us, length us, event | category | flops | bytes accessed | tf_op | source)
XLA Modules:
  0.0 34.1 jit_solution(16706476236075172562)
XLA Ops:
  0.6 31.8 %shard_map.75 = (f32[128,128]{1,0:T(8,128)S(1)}, f32[4,512,128]{2,1,0:T(8,128)S(1)}, f32[768,128]{1,0:T(8,128)S(1)}, f32[8,128]{1,0:T(8,128)S(1)}) custom-call(s32[1,4]{1,0:T(1,128)} %lens_in.1, bf16[128,768]{1,0:T(8,128)(2,1)} %bitcast.6, bf16[768,128]{1,0:T(8,128)(2,1)} %proj_in.1, bf16[4,512,768]{2,1,0:T(8,128)(2,1)} %bitcast.5), custom_call_target="tpu_custom_call" | custom-call | tf_op jit(solution)/shard_map/pallas_call | solution.py:338
  32.5 1.6 %shard_map.76 = (f32[128,128]{1,0:T(8,128)}, f32[4,512,128]{2,1,0:T(8,128)}, f32[768,128]{1,0:T(8,128)}, f32[1,1]{1,0:T(1,128)}) custom-call(f32[128,128]{1,0:T(8,128)S(1)} %get-tuple-element.12.qg, f32[4,512,128]{2,1,0:T(8,128)S(1)} %get-tuple-element.13.pg, f32[768,128]{1,0:T(8,128)S(1)} %get-tuple-element.14.wg, f32[8,128]{1,0:T(8,128)S(1)} %get-tuple-element.15.loss), custom_call_target="tpu_custom_call" | custom-call | tf_op jit(solution)/shard_map/pallas_call | solution.py:387

commit v2 on v1

--- a/solution.py
+++ b/solution.py
@@ -154,9 +154,21 @@
     tok[0] = jnp.dot(hid[ntp : ntp + ntok, :], proj[...], preferred_element_type=F32).astype(BF16)
     pl.semaphore_wait(barrier, greeted)
     tok_copies = share(lambda k: tok.at[0], lambda k: tok.at[k], tok_s, tok_r, blk_peer, nblk)
-    hid_copies = share(
-        lambda k: qhid_in, lambda k: hid.at[pl.ds(ntp + k * ntok, ntok)], hid_s, hid_r, blk_peer, nblk
-    )
+    half = ntok // 2
+
+    def send_hid(n, k, slot, source, piece):
+        start = piece * half
+        copy = pltpu.make_async_remote_copy(
+            src_ref=hid.at[pl.ds(ntp + source * ntok + start, half)],
+            dst_ref=hid.at[pl.ds(ntp + slot * ntok + start, half)],
+            send_sem=hid_s.at[n], recv_sem=hid_r.at[n], device_id=blk_peer(k), device_id_type=MESH,
+        )
+        copy.start()
+        return copy
+
+    relayed = paired and nblk == 4
+    hid_plan = [(k, k, 0, (k + 1 + turn) % 2) for turn in range(2) for k in range(1, 3 if relayed else nblk)]
+    hid_copies = [send_hid(n, *plan) for n, plan in enumerate(hid_plan)]
     if nz > 2:
         tell(1)
 
@@ -207,6 +219,11 @@
             hear(step)
             if step + 1 < nz - 1:
                 tell(step + 1)
+    relays = []
+    if relayed:
+        for n, (k, source) in enumerate(((2, 1), (1, 2))):
+            hid_copies[n].wait_recv()
+            relays.append(send_hid(len(hid_plan) + n, k, 3, source, n))
     for copy in sc_copies:
         copy.wait_recv()
 
@@ -229,7 +246,7 @@
     grads[:, ntp:] = qg_b
     for k in range(1, nblk):
         qsend[k] = qg_b[:, k * ntok : (k + 1) * ntok]
-    qg_copies = share(lambda k: qsend.at[k], lambda k: qrecv.at[k], qg_s, qg_r, blk_peer, nblk)
+    qg_copies = []
 
     for p in range(npass):
         side = (every_t * factor[p : p + 1]).astype(BF16)
@@ -243,8 +260,9 @@
     lo_c[core] = jnp.broadcast_to(jnp.sum(gap, 1, keepdims=True), lo_c.shape[1:])
     lc_copies = share(lambda k: lo_c.at[core], lambda k: lo_c.at[core], lc_s, lc_r, core_peer, ncore)
 
-    for copy in hid_copies:
+    for copy in (hid_copies[2:] if relayed else hid_copies) + relays:
         copy.wait_recv()
+    hid_copies = hid_copies + relays
     ws_copies = []
     for h in range(parts):
         w = jnp.dot(grads[...], hid[:, h * cols : (h + 1) * cols], preferred_element_type=F32)
@@ -255,25 +273,25 @@
             lambda k: wsend.at[h, a_index(k)], lambda k: wrecv.at[h, me_a], ws_s.at[h], ws_r.at[h], a_peer, na
         ))
 
+    qg_copies = share(lambda k: qsend.at[k], lambda k: qrecv.at[k], qg_s, qg_r, blk_peer, nblk)
     for copy in lc_copies:
         copy.wait_recv()
     lo_z[zed] = jnp.sum(lo_c[...], 0)
     lz_copies = share(lambda k: lo_z.at[zed], lambda k: lo_z.at[zed], lz_s, lz_r, z_peer, nz)
+    z_copies = []
+    for h in range(parts):
+        for copy in ws_copies[h]:
+            copy.wait_recv()
+        zbuf[h, zed] = jnp.sum(wrecv[h].astype(F32), 0).astype(BF16)
+        z_copies.append(share(
+            lambda k: zbuf.at[h, zed], lambda k: zbuf.at[h, zed], z_s.at[h], z_r.at[h], z_peer, nz
+        ))
     for copy in qg_copies:
         copy.wait_recv()
     mine_t = grads[:, ntp : ntp + ntok].astype(F32)
     for k in range(1, nblk):
         mine_t = mine_t + qrecv[k].astype(F32)
     qg_out[...] = mine_t.T
-
-    z_copies = []
-    for h in range(parts):
-        for copy in ws_copies[h]:
-            copy.wait_recv()
-        zbuf[h, zed] = jnp.sum(wrecv[h].astype(F32), 0).astype(BF16)
-        z_copies.append(share(
-            lambda k: zbuf.at[h, zed], lambda k: zbuf.at[h, zed], z_s.at[h], z_r.at[h], z_peer, nz
-        ))
     for copy in lz_copies:
         copy.wait_recv()
     loss_out[...] = jnp.sum(lo_z[...], 0) / total
@@ -331,8 +349,9 @@
     sem = lambda *n: pltpu.SemaphoreType.DMA(tuple(max(i, 1) for i in n))
     flag = pltpu.SemaphoreType.REGULAR((max(nz - 2, 1),))
     pairs = []
-    for n in (nblk, nblk, nblk, ncore, nz, nblk):
+    for n in (nblk, nblk, ncore, nz, nblk):
         pairs += [sem(n - 1), sem(n - 1)]
+    pairs[2:2] = [sem(2 * nblk), sem(2 * nblk)]
     for n in (na, nz, na):
         pairs += [sem(parts, n - 1), sem(parts, n - 1)]
     held = pl.pallas_call(

time: 34.3 us -> 31.1 us (0.907)
  Pallas kernels: 33.5 us -> 30.3 us
    pallas_call x1, Pallas kernels: 31.8 us -> 28.6 us  [shards(): pl.pallas_call(functools.partial(kernel, dims), out_shape=(pltpu.VMEM((nt...]
where the time goes in v2:
time: 31.1 us; the launch traced here: 30.9 us
  Pallas kernels  30.3 us (97%)
  between operations  0.64 us (2%)
    pallas_call x1, Pallas kernels, shards(): pl.pallas_call(functools.partial(kernel, dims), out_shape=(pltpu.VMEM((nt...  28.6 us
    pallas_call x1, Pallas kernels, shards(): pl.pallas_call(write_out, out_shape=(jax.ShapeDtypeStruct((ntok, dim), F3...  1.65 us

profile of v2, /device:TPU:0, one launch (start us, length us, event | category | flops | bytes accessed | tf_op | source)
XLA Modules:
  0.0 30.9 jit_solution(16462829518245404712)
XLA Ops:
  0.6 28.6 %shard_map.75 = (f32[128,128]{1,0:T(8,128)S(1)}, f32[4,512,128]{2,1,0:T(8,128)S(1)}, f32[768,128]{1,0:T(8,128)S(1)}, f32[8,128]{1,0:T(8,128)S(1)}) custom-call(s32[1,4]{1,0:T(1,128)} %lens_in.1, bf16[128,768]{1,0:T(8,128)(2,1)} %bitcast.6, bf16[768,128]{1,0:T(8,128)(2,1)} %proj_in.1, bf16[4,512,768]{2,1,0:T(8,128)(2,1)} %bitcast.5), custom_call_target="tpu_custom_call" | custom-call | tf_op jit(solution)/shard_map/pallas_call | solution.py:357
  29.3 1.6 %shard_map.76 = (f32[128,128]{1,0:T(8,128)}, f32[4,512,128]{2,1,0:T(8,128)}, f32[768,128]{1,0:T(8,128)}, f32[1,1]{1,0:T(1,128)}) custom-call(f32[128,128]{1,0:T(8,128)S(1)} %get-tuple-element.12.qg, f32[4,512,128]{2,1,0:T(8,128)S(1)} %get-tuple-element.13.pg, f32[768,128]{1,0:T(8,128)S(1)} %get-tuple-element.14.wg, f32[8,128]{1,0:T(8,128)S(1)} %get-tuple-element.15.loss), custom_call_target="tpu_custom_call" | custom-call | tf_op jit(solution)/shard_map/pallas_call | solution.py:406

commit v3 on v2

--- a/solution.py
+++ b/solution.py
@@ -89,16 +89,21 @@
     def z_next(step):
         return (blk, (zed + step) * ncore + core)
 
+    def start_copy(src, dst, send, recv, device):
+        copy = pltpu.make_async_remote_copy(
+            src_ref=src, dst_ref=dst, send_sem=send, recv_sem=recv, device_id=device, device_id_type=MESH
+        )
+        copy.start()
+        return copy
+
+    def bytes_of(view, send, recv):
+        return pltpu.make_async_remote_copy(
+            src_ref=view, dst_ref=view, send_sem=send, recv_sem=recv, device_id=a_peer(1), device_id_type=MESH
+        )
+
     def share(src, dst, send, recv, peer, count):
-        copies = []
         for k in range(1, count):
-            copy = pltpu.make_async_remote_copy(
-                src_ref=src(k), dst_ref=dst(k), send_sem=send.at[k - 1], recv_sem=recv.at[k - 1],
-                device_id=peer(k), device_id_type=MESH,
-            )
-            copy.start()
-            copies.append(copy)
-        return copies
+            start_copy(src(k), dst(k), send, recv, peer(k))
 
     def tell(step):
         @pl.when((zed >= step) & (zed + 1 < nz))
@@ -153,22 +158,21 @@
     loads[1].wait()
     tok[0] = jnp.dot(hid[ntp : ntp + ntok, :], proj[...], preferred_element_type=F32).astype(BF16)
     pl.semaphore_wait(barrier, greeted)
-    tok_copies = share(lambda k: tok.at[0], lambda k: tok.at[k], tok_s, tok_r, blk_peer, nblk)
+    tok_copies = [start_copy(tok.at[0], tok.at[k], tok_s.at[k - 1], tok_r.at[k - 1], blk_peer(k)) for k in range(1, nblk)]
     half = ntok // 2
 
-    def send_hid(n, k, slot, source, piece):
+    def send_hid(k, slot, source, piece, recv):
         start = piece * half
-        copy = pltpu.make_async_remote_copy(
-            src_ref=hid.at[pl.ds(ntp + source * ntok + start, half)],
-            dst_ref=hid.at[pl.ds(ntp + slot * ntok + start, half)],
-            send_sem=hid_s.at[n], recv_sem=hid_r.at[n], device_id=blk_peer(k), device_id_type=MESH,
+        start_copy(
+            hid.at[pl.ds(ntp + source * ntok + start, half)], hid.at[pl.ds(ntp + slot * ntok + start, half)],
+            hid_s.at[0], recv, blk_peer(k),
         )
-        copy.start()
-        return copy
 
     relayed = paired and nblk == 4
-    hid_plan = [(k, k, 0, (k + 1 + turn) % 2) for turn in range(2) for k in range(1, 3 if relayed else nblk)]
-    hid_copies = [send_hid(n, *plan) for n, plan in enumerate(hid_plan)]
+    near = 3 if relayed else nblk
+    for turn in range(2):
+        for k in range(1, near):
+            send_hid(k, k, 0, (k + 1 + turn) % 2, hid_r.at[turn])
     if nz > 2:
         tell(1)
 
@@ -209,9 +213,15 @@
     pooled = temper * (tops[...] * (1.0 / temper) + jnp.log(sums[...]) - log_size)
     own = split_dot(pooled, pick[...], 3)
     sc[0] = own
-    sc_copies = share(lambda k: sc.at[0], lambda k: sc.at[k], sc_s, sc_r, blk_peer, nblk)
+    share(lambda k: sc.at[0], lambda k: sc.at[k], sc_s.at[0], sc_r.at[0], blk_peer, nblk)
+    sc_all = bytes_of(sc.at[pl.ds(0, nblk - 1)], sc_s.at[0], sc_r.at[0])
     inv = 1.0 / sums[...]
     every_t = jnp.concatenate([tok[k].astype(F32).T for k in range(nblk)], 1)
+    if nblk > 1:
+        bytes_of(hid.at[pl.ds(ntp, (near - 1) * half)], hid_s.at[0], hid_r.at[0]).wait_recv()
+    if relayed:
+        send_hid(2, 3, 1, 0, hid_r.at[1])
+        send_hid(1, 3, 2, 1, hid_r.at[1])
     for p in range(npass):
         reach[p] = jnp.dot(ptok_t[p], expo[p], preferred_element_type=F32)
     if nz > 2:
@@ -219,13 +229,8 @@
             hear(step)
             if step + 1 < nz - 1:
                 tell(step + 1)
-    relays = []
-    if relayed:
-        for n, (k, source) in enumerate(((2, 1), (1, 2))):
-            hid_copies[n].wait_recv()
-            relays.append(send_hid(len(hid_plan) + n, k, 3, source, n))
-    for copy in sc_copies:
-        copy.wait_recv()
+    if nblk > 1:
+        sc_all.wait_recv()
 
     score = sc[...]
     row = rows_iota(score.shape, 1)
@@ -246,7 +251,6 @@
     grads[:, ntp:] = qg_b
     for k in range(1, nblk):
         qsend[k] = qg_b[:, k * ntok : (k + 1) * ntok]
-    qg_copies = []
 
     for p in range(npass):
         side = (every_t * factor[p : p + 1]).astype(BF16)
@@ -258,63 +262,64 @@
     aim = jnp.sum(jnp.sum(jnp.where(hit, score, 0.0), 0), 0, keepdims=True)
     gap = jnp.where(rows_iota(lse.shape, 1) < nq_all, lse - aim, 0.0)
     lo_c[core] = jnp.broadcast_to(jnp.sum(gap, 1, keepdims=True), lo_c.shape[1:])
-    lc_copies = share(lambda k: lo_c.at[core], lambda k: lo_c.at[core], lc_s, lc_r, core_peer, ncore)
-
-    for copy in (hid_copies[2:] if relayed else hid_copies) + relays:
-        copy.wait_recv()
-    hid_copies = hid_copies + relays
-    ws_copies = []
+    share(lambda k: lo_c.at[core], lambda k: lo_c.at[core], lc_s.at[0], lc_r.at[0], core_peer, ncore)
+    lc_all = bytes_of(lo_c.at[pl.ds(0, ncore - 1)], lc_s.at[0], lc_r.at[0])
+
+    late = near - 1 + 2 * relayed
+    if nblk > 1:
+        bytes_of(hid.at[pl.ds(ntp, late * half)], hid_s.at[0], hid_r.at[1]).wait_recv()
     for h in range(parts):
         w = jnp.dot(grads[...], hid[:, h * cols : (h + 1) * cols], preferred_element_type=F32)
         w = w.T.astype(BF16).reshape(na, cols // na, dim)
         wsend[h] = w
         wrecv[h, me_a] = wsend[h, me_a]
-        ws_copies.append(share(
-            lambda k: wsend.at[h, a_index(k)], lambda k: wrecv.at[h, me_a], ws_s.at[h], ws_r.at[h], a_peer, na
-        ))
-
-    qg_copies = share(lambda k: qsend.at[k], lambda k: qrecv.at[k], qg_s, qg_r, blk_peer, nblk)
-    for copy in lc_copies:
-        copy.wait_recv()
+        share(lambda k: wsend.at[h, a_index(k)], lambda k: wrecv.at[h, me_a], ws_s.at[0], ws_r.at[h], a_peer, na)
+
+    share(lambda k: qsend.at[k], lambda k: qrecv.at[k], qg_s.at[0], qg_r.at[0], blk_peer, nblk)
+    qg_all = bytes_of(qrecv.at[pl.ds(0, nblk - 1)], qg_s.at[0], qg_r.at[0])
+    if ncore > 1:
+        lc_all.wait_recv()
     lo_z[zed] = jnp.sum(lo_c[...], 0)
-    lz_copies = share(lambda k: lo_z.at[zed], lambda k: lo_z.at[zed], lz_s, lz_r, z_peer, nz)
-    z_copies = []
+    share(lambda k: lo_z.at[zed], lambda k: lo_z.at[zed], lz_s.at[0], lz_r.at[0], z_peer, nz)
+    lz_all = bytes_of(lo_z.at[pl.ds(0, nz - 1)], lz_s.at[0], lz_r.at[0])
     for h in range(parts):
-        for copy in ws_copies[h]:
-            copy.wait_recv()
+        if na > 1:
+            bytes_of(wrecv.at[h, pl.ds(0, na - 1)], ws_s.at[0], ws_r.at[h]).wait_recv()
         zbuf[h, zed] = jnp.sum(wrecv[h].astype(F32), 0).astype(BF16)
-        z_copies.append(share(
-            lambda k: zbuf.at[h, zed], lambda k: zbuf.at[h, zed], z_s.at[h], z_r.at[h], z_peer, nz
-        ))
-    for copy in qg_copies:
-        copy.wait_recv()
+        share(lambda k: zbuf.at[h, zed], lambda k: zbuf.at[h, zed], z_s.at[0], z_r.at[h], z_peer, nz)
+    if nblk > 1:
+        qg_all.wait_recv()
     mine_t = grads[:, ntp : ntp + ntok].astype(F32)
     for k in range(1, nblk):
         mine_t = mine_t + qrecv[k].astype(F32)
     qg_out[...] = mine_t.T
-    for copy in lz_copies:
-        copy.wait_recv()
+    if nz > 1:
+        lz_all.wait_recv()
     loss_out[...] = jnp.sum(lo_z[...], 0) / total
-    c_copies = []
     for h in range(parts):
-        for copy in z_copies[h]:
-            copy.wait_recv()
+        if nz > 1:
+            bytes_of(zbuf.at[h, pl.ds(0, nz - 1)], z_s.at[0], z_r.at[h]).wait_recv()
         cbuf[h, me_a] = jnp.sum(zbuf[h].astype(F32), 0).astype(BF16)
-        c_copies.append(share(
-            lambda k: cbuf.at[h, me_a], lambda k: cbuf.at[h, me_a], c_s.at[h], c_r.at[h], a_peer, na
-        ))
-    for copy in tok_copies + hid_copies + sc_copies + qg_copies + lc_copies + lz_copies:
+        share(lambda k: cbuf.at[h, me_a], lambda k: cbuf.at[h, me_a], c_s.at[0], c_r.at[h], a_peer, na)
+    for copy in tok_copies:
         copy.wait_send()
+    if nblk > 1:
+        bytes_of(hid.at[pl.ds(ntp, (2 * (near - 1) + 2 * relayed) * half)], hid_s.at[0], hid_r.at[0]).wait_send()
+        sc_all.wait_send()
+        qg_all.wait_send()
+    if ncore > 1:
+        lc_all.wait_send()
+    if na > 1:
+        bytes_of(wsend.at[:, pl.ds(0, na - 1)], ws_s.at[0], ws_r.at[0]).wait_send()
+    if nz > 1:
+        lz_all.wait_send()
+        bytes_of(zbuf.at[:, pl.ds(0, nz - 1)], z_s.at[0], z_r.at[0]).wait_send()
     for h in range(parts):
-        for copy in ws_copies[h] + z_copies[h]:
-            copy.wait_send()
-    for h in range(parts):
-        for copy in c_copies[h]:
-            copy.wait_recv()
+        if na > 1:
+            bytes_of(cbuf.at[h, pl.ds(0, na - 1)], c_s.at[0], c_r.at[h]).wait_recv()
         wg_out[h * cols : (h + 1) * cols, :] = cbuf[h].astype(F32).reshape(cols, dim)
-    for h in range(parts):
-        for copy in c_copies[h]:
-            copy.wait_send()
+    if na > 1:
+        bytes_of(cbuf.at[:, pl.ds(0, na - 1)], c_s.at[0], c_r.at[0]).wait_send()
 
 
 def write_out(qg, pg, wg, loss, qg_out, pg_out, wg_out, loss_out, sem):
@@ -348,12 +353,9 @@
     vmem = pl.BlockSpec(memory_space=pltpu.VMEM)
     sem = lambda *n: pltpu.SemaphoreType.DMA(tuple(max(i, 1) for i in n))
     flag = pltpu.SemaphoreType.REGULAR((max(nz - 2, 1),))
-    pairs = []
-    for n in (nblk, nblk, ncore, nz, nblk):
-        pairs += [sem(n - 1), sem(n - 1)]
-    pairs[2:2] = [sem(2 * nblk), sem(2 * nblk)]
-    for n in (na, nz, na):
-        pairs += [sem(parts, n - 1), sem(parts, n - 1)]
+    pairs = [sem(nblk - 1), sem(nblk - 1), sem(1), sem(2)]
+    pairs += [sem(1)] * 8
+    pairs += [sem(1), sem(parts)] * 3
     held = pl.pallas_call(
         functools.partial(kernel, dims),
         out_shape=(

time: 31.1 us -> 30.1 us (0.968)
  Pallas kernels: 30.3 us -> 29.3 us
    pallas_call x1, Pallas kernels: 28.6 us -> 27.7 us  [shards(): pl.pallas_call(functools.partial(kernel, dims), out_shape=(pltpu.VMEM((nt...]
where the time goes in v3:
time: 30.1 us; the launch traced here: 30 us
  Pallas kernels  29.3 us (97%)
  between operations  0.64 us (2%)
    pallas_call x1, Pallas kernels, shards(): pl.pallas_call(functools.partial(kernel, dims), out_shape=(pltpu.VMEM((nt...  27.7 us
    pallas_call x1, Pallas kernels, shards(): pl.pallas_call(write_out, out_shape=(jax.ShapeDtypeStruct((ntok, dim), F3...  1.65 us

profile of v3, /device:TPU:0, one launch (start us, length us, event | category | flops | bytes accessed | tf_op | source)
XLA Modules:
  0.0 30.0 jit_solution(8393012562379241028)
XLA Ops:
  0.6 27.7 %shard_map.75 = (f32[128,128]{1,0:T(8,128)S(1)}, f32[4,512,128]{2,1,0:T(8,128)S(1)}, f32[768,128]{1,0:T(8,128)S(1)}, f32[8,128]{1,0:T(8,128)S(1)}) custom-call(s32[1,4]{1,0:T(1,128)} %lens_in.1, bf16[128,768]{1,0:T(8,128)(2,1)} %bitcast.6, bf16[768,128]{1,0:T(8,128)(2,1)} %proj_in.1, bf16[4,512,768]{2,1,0:T(8,128)(2,1)} %bitcast.5), custom_call_target="tpu_custom_call" | custom-call | tf_op jit(solution)/shard_map/pallas_call | solution.py:359
  28.3 1.6 %shard_map.76 = (f32[128,128]{1,0:T(8,128)}, f32[4,512,128]{2,1,0:T(8,128)}, f32[768,128]{1,0:T(8,128)}, f32[1,1]{1,0:T(1,128)}) custom-call(f32[128,128]{1,0:T(8,128)S(1)} %get-tuple-element.12.qg, f32[4,512,128]{2,1,0:T(8,128)S(1)} %get-tuple-element.13.pg, f32[768,128]{1,0:T(8,128)S(1)} %get-tuple-element.14.wg, f32[8,128]{1,0:T(8,128)S(1)} %get-tuple-element.15.loss), custom_call_target="tpu_custom_call" | custom-call | tf_op jit(solution)/shard_map/pallas_call | solution.py:408

commit v4 on v3

--- a/solution.py
+++ b/solution.py
@@ -11,6 +11,7 @@
 F32 = jnp.float32
 BF16 = jnp.bfloat16
 NT = (((1,), (1,)), ((), ()))
+TN = (((0,), (0,)), ((), ()))
 
 temper = 0.5
 LANES = 128
@@ -34,7 +35,7 @@
 
 def kernel(
     dims, lens_in, qhid_in, proj_in, phid, qg_out, pg_v, wg_out, loss_out,
-    lens, proj, pick, spread, tok, ptok, ptok_t, hid, expo, reach, grads, tops, sums, sc, lo_c, lo_z, qsend, qrecv,
+    lens, proj, pick, spread, tok, ptok, ptok_t, hid, expo, reach, grads, drawn, tops, sums, sc, lo_c, lo_z, qsend, qrecv,
     wsend, wrecv, zbuf, cbuf,
     in_sem, up, down, tok_s, tok_r, hid_s, hid_r, sc_s, sc_r, lc_s, lc_r, lz_s, lz_r, qg_s, qg_r, ws_s, ws_r,
     z_s, z_r, c_s, c_r,
@@ -44,6 +45,7 @@
     nqi = nblk * ntok
     nq_all = nblk * nquery
     ntp = npass * plen
+    nfac = npass * nqi
     nz = nrep // ncore
     na = nblk * ncore
     hidden, dim = proj.shape
@@ -57,13 +59,13 @@
     zed = rep // ncore
     me_a = blk * ncore + core
 
-    def blk_at(k):
-        if not paired:
-            return lax.rem(blk + k, nblk)
+    def mixed(index, k, count):
+        if count & (count - 1):
+            return lax.rem(index + k, count)
         out = 0
         bit = 1
-        while bit < nblk:
-            out = out + lax.rem(blk // bit + k // bit, 2) * bit
+        while bit < count:
+            out = out + lax.rem(index // bit + k // bit, 2) * bit
             bit *= 2
         return out
 
@@ -71,20 +73,20 @@
         return slots ^ blk if paired else lax.rem(blk + nblk - slots, nblk)
 
     def blk_peer(k):
-        return (blk_at(k), rep)
+        return (mixed(blk, k, nblk), rep)
 
     def core_peer(k):
         return (blk, zed * ncore + lax.rem(core + k, ncore))
 
     def a_index(k):
-        return lax.rem(me_a + k, na)
+        return mixed(me_a, k, na)
 
     def a_peer(k):
         other = a_index(k)
         return (other // ncore, zed * ncore + lax.rem(other, ncore))
 
     def z_peer(k):
-        return (blk, lax.rem(zed + k, nz) * ncore + core)
+        return (blk, mixed(zed, k, nz) * ncore + core)
 
     def z_next(step):
         return (blk, (zed + step) * ncore + core)
@@ -102,7 +104,7 @@
         )
 
     def share(src, dst, send, recv, peer, count):
-        for k in range(1, count):
+        for k in range(count - 1, 0, -1):
             start_copy(src(k), dst(k), send, recv, peer(k))
 
     def tell(step):
@@ -124,7 +126,7 @@
             pl.semaphore_wait(down.at[step - 1], 1)
 
     barrier = pltpu.get_barrier_semaphore()
-    for k in range(1, na):
+    for k in range(na - 1, 0, -1):
         pl.semaphore_signal(barrier, inc=1, device_id=a_peer(k), device_id_type=MESH)
 
     @pl.when(zed + 1 < nz)
@@ -158,21 +160,38 @@
     loads[1].wait()
     tok[0] = jnp.dot(hid[ntp : ntp + ntok, :], proj[...], preferred_element_type=F32).astype(BF16)
     pl.semaphore_wait(barrier, greeted)
-    tok_copies = [start_copy(tok.at[0], tok.at[k], tok_s.at[k - 1], tok_r.at[k - 1], blk_peer(k)) for k in range(1, nblk)]
+    tok_copies = [start_copy(tok.at[0], tok.at[k], tok_s.at[k - 1], tok_r.at[k - 1], blk_peer(k)) for k in range(nblk - 1, 0, -1)][::-1]
+    relayed = paired and nblk == 4
     half = ntok // 2
 
-    def send_hid(k, slot, source, piece, recv):
-        start = piece * half
+    def send_hid(h, k, slot, source, start, count, recv):
+        here = pl.ds(h * cols, cols)
         start_copy(
-            hid.at[pl.ds(ntp + source * ntok + start, half)], hid.at[pl.ds(ntp + slot * ntok + start, half)],
-            hid_s.at[0], recv, blk_peer(k),
+            hid.at[pl.ds(ntp + source * ntok + start, count), here],
+            hid.at[pl.ds(ntp + slot * ntok + start, count), here],
+            hid_s.at[0], hid_r.at[recv], blk_peer(k),
         )
 
-    relayed = paired and nblk == 4
-    near = 3 if relayed else nblk
-    for turn in range(2):
-        for k in range(1, near):
-            send_hid(k, k, 0, (k + 1 + turn) % 2, hid_r.at[turn])
+    def hid_bytes(h, rows, recv):
+        return bytes_of(hid.at[pl.ds(ntp, rows), pl.ds(h * cols, cols)], hid_s.at[0], hid_r.at[recv])
+
+    def relay(h):
+        if relayed:
+            hid_bytes(h, 2 * half, h).wait_recv()
+            send_hid(h, 2, 3, 1, 0, half, parts + h)
+            send_hid(h, 1, 3, 2, half, half, parts + h)
+
+    if relayed:
+        for turn in range(2):
+            for h in range(parts):
+                for k in (1, 2):
+                    send_hid(h, k, k, 0, (k + 1 + turn) % 2 * half, half, turn * parts + h)
+        late_rows, sent_rows = 4 * half, 6 * half
+    else:
+        for h in range(parts):
+            for k in range(1, nblk):
+                send_hid(h, k, k, 0, 0, ntok, parts + h)
+        late_rows = sent_rows = (nblk - 1) * ntok
     if nz > 2:
         tell(1)
 
@@ -200,7 +219,17 @@
             tops[pl.ds(p, 1), here] = top
             sums[pl.ds(p, 1), here] = jnp.sum(e, 0, keepdims=True)
 
+    def collect(first, count):
+        width = count * ntok
+        for p in range(npass):
+            m = lax.dot_general(
+                expo[p, :, pl.ds(first * ntok, width)], hid[p * plen : (p + 1) * plen, :], TN,
+                preferred_element_type=F32,
+            )
+            drawn[pl.ds(p * nqi + first * ntok, width), :] = m.astype(BF16)
+
     forward(0, 1)
+    collect(0, 1)
     for k in range(1, nblk - 1):
         tok_copies[k - 1].wait_recv()
     if nblk > 2:
@@ -217,13 +246,16 @@
     sc_all = bytes_of(sc.at[pl.ds(0, nblk - 1)], sc_s.at[0], sc_r.at[0])
     inv = 1.0 / sums[...]
     every_t = jnp.concatenate([tok[k].astype(F32).T for k in range(nblk)], 1)
-    if nblk > 1:
-        bytes_of(hid.at[pl.ds(ntp, (near - 1) * half)], hid_s.at[0], hid_r.at[0]).wait_recv()
-    if relayed:
-        send_hid(2, 3, 1, 0, hid_r.at[1])
-        send_hid(1, 3, 2, 1, hid_r.at[1])
+    relay(0)
+    later = list(range(1, parts))
     for p in range(npass):
         reach[p] = jnp.dot(ptok_t[p], expo[p], preferred_element_type=F32)
+        if later and p % 2 == 0:
+            relay(later.pop(0))
+    for h in later:
+        relay(h)
+    if nblk > 1:
+        collect(1, nblk - 1)
     if nz > 2:
         for step in range(1, nz - 1):
             hear(step)
@@ -244,19 +276,29 @@
     dscore = (jnp.exp(sc[0] - lse) - mine.astype(F32)) / total
     factor = split_dot(dscore, spread[...], 3) * inv
 
+    for p in range(npass):
+        grads[:, p * nqi : (p + 1) * nqi] = (every_t * factor[p : p + 1]).astype(BF16)
     qg_t = reach[0] * factor[0:1]
     for p in range(1, npass):
         qg_t = qg_t + reach[p] * factor[p : p + 1]
     qg_b = qg_t.astype(BF16)
-    grads[:, ntp:] = qg_b
+    grads[:, nfac:] = qg_b
     for k in range(1, nblk):
         qsend[k] = qg_b[:, k * ntok : (k + 1) * ntok]
 
-    for p in range(npass):
-        side = (every_t * factor[p : p + 1]).astype(BF16)
-        g = lax.dot_general(expo[p], side, NT, preferred_element_type=F32)
-        pg_v[p] = g
-        grads[:, p * plen : (p + 1) * plen] = g.astype(BF16).T
+    for h in range(parts):
+        here = slice(h * cols, (h + 1) * cols)
+        w = jnp.dot(grads[:, :nfac], drawn[:, here], preferred_element_type=F32)
+        if nblk > 1:
+            hid_bytes(h, late_rows, parts + h).wait_recv()
+        w = w + jnp.dot(grads[:, nfac:], hid[ntp:, here], preferred_element_type=F32)
+        w = w.T.astype(BF16).reshape(na, cols // na, dim)
+        wsend[h] = w
+        wrecv[h, me_a] = wsend[h, me_a]
+        share(lambda k: wsend.at[h, a_index(k)], lambda k: wrecv.at[h, me_a], ws_s.at[0], ws_r.at[h], a_peer, na)
+
+    share(lambda k: qsend.at[k], lambda k: qrecv.at[k], qg_s.at[0], qg_r.at[0], blk_peer, nblk)
+    qg_all = bytes_of(qrecv.at[pl.ds(0, nblk - 1)], qg_s.at[0], qg_r.at[0])
 
     hit = live & (slot_owner(slot) * npass + row == lane)
     aim = jnp.sum(jnp.sum(jnp.where(hit, score, 0.0), 0), 0, keepdims=True)
@@ -264,19 +306,10 @@
     lo_c[core] = jnp.broadcast_to(jnp.sum(gap, 1, keepdims=True), lo_c.shape[1:])
     share(lambda k: lo_c.at[core], lambda k: lo_c.at[core], lc_s.at[0], lc_r.at[0], core_peer, ncore)
     lc_all = bytes_of(lo_c.at[pl.ds(0, ncore - 1)], lc_s.at[0], lc_r.at[0])
-
-    late = near - 1 + 2 * relayed
-    if nblk > 1:
-        bytes_of(hid.at[pl.ds(ntp, late * half)], hid_s.at[0], hid_r.at[1]).wait_recv()
-    for h in range(parts):
-        w = jnp.dot(grads[...], hid[:, h * cols : (h + 1) * cols], preferred_element_type=F32)
-        w = w.T.astype(BF16).reshape(na, cols // na, dim)
-        wsend[h] = w
-        wrecv[h, me_a] = wsend[h, me_a]
-        share(lambda k: wsend.at[h, a_index(k)], lambda k: wrecv.at[h, me_a], ws_s.at[0], ws_r.at[h], a_peer, na)
-
-    share(lambda k: qsend.at[k], lambda k: qrecv.at[k], qg_s.at[0], qg_r.at[0], blk_peer, nblk)
-    qg_all = bytes_of(qrecv.at[pl.ds(0, nblk - 1)], qg_s.at[0], qg_r.at[0])
+    for p in range(npass):
+        pg_v[p] = lax.dot_general(
+            expo[p], grads[:, p * nqi : (p + 1) * nqi], NT, preferred_element_type=F32
+        )
     if ncore > 1:
         lc_all.wait_recv()
     lo_z[zed] = jnp.sum(lo_c[...], 0)
@@ -289,7 +322,7 @@
         share(lambda k: zbuf.at[h, zed], lambda k: zbuf.at[h, zed], z_s.at[0], z_r.at[h], z_peer, nz)
     if nblk > 1:
         qg_all.wait_recv()
-    mine_t = grads[:, ntp : ntp + ntok].astype(F32)
+    mine_t = grads[:, nfac : nfac + ntok].astype(F32)
     for k in range(1, nblk):
         mine_t = mine_t + qrecv[k].astype(F32)
     qg_out[...] = mine_t.T
@@ -304,7 +337,7 @@
     for copy in tok_copies:
         copy.wait_send()
     if nblk > 1:
-        bytes_of(hid.at[pl.ds(ntp, (2 * (near - 1) + 2 * relayed) * half)], hid_s.at[0], hid_r.at[0]).wait_send()
+        bytes_of(hid.at[pl.ds(ntp, sent_rows)], hid_s.at[0], hid_r.at[0]).wait_send()
         sc_all.wait_send()
         qg_all.wait_send()
     if ncore > 1:
@@ -353,7 +386,7 @@
     vmem = pl.BlockSpec(memory_space=pltpu.VMEM)
     sem = lambda *n: pltpu.SemaphoreType.DMA(tuple(max(i, 1) for i in n))
     flag = pltpu.SemaphoreType.REGULAR((max(nz - 2, 1),))
-    pairs = [sem(nblk - 1), sem(nblk - 1), sem(1), sem(2)]
+    pairs = [sem(nblk - 1), sem(nblk - 1), sem(1), sem(2 * parts)]
     pairs += [sem(1)] * 8
     pairs += [sem(1), sem(parts)] * 3
     held = pl.pallas_call(
@@ -379,7 +412,8 @@
             pltpu.VMEM((ntp + nqi, hidden), BF16),
             pltpu.VMEM((npass, plen, nqi), BF16),
             pltpu.VMEM((npass, dim, nqi), F32),
-            pltpu.VMEM((dim, ntp + nqi), BF16),
+            pltpu.VMEM((dim, npass * nqi + nqi), BF16),
+            pltpu.VMEM((npass * nqi, hidden), BF16),
             pltpu.VMEM((ppad, nqi), F32),
             pltpu.VMEM((ppad, nqi), F32),
             pltpu.VMEM((nblk, ppad, qpad), F32),

time: 30.1 us -> 29.5 us (0.980)
  Pallas kernels: 29.3 us -> 28.7 us
    pallas_call x1, Pallas kernels: 27.7 us -> 27.1 us  [shards(): pl.pallas_call(functools.partial(kernel, dims), out_shape=(pltpu.VMEM((nt...]
where the time goes in v4:
time: 29.5 us; the launch traced here: 29.4 us
  Pallas kernels  28.7 us (97%)
  between operations  0.64 us (2%)
    pallas_call x1, Pallas kernels, shards(): pl.pallas_call(functools.partial(kernel, dims), out_shape=(pltpu.VMEM((nt...  27.1 us
    pallas_call x1, Pallas kernels, shards(): pl.pallas_call(write_out, out_shape=(jax.ShapeDtypeStruct((ntok, dim), F3...  1.65 us

profile of v4, /device:TPU:0, one launch (start us, length us, event | category | flops | bytes accessed | tf_op | source)
XLA Modules:
  0.0 29.4 jit_solution(3441997060240998686)
XLA Ops:
  0.6 27.1 %shard_map.75 = (f32[128,128]{1,0:T(8,128)S(1)}, f32[4,512,128]{2,1,0:T(8,128)S(1)}, f32[768,128]{1,0:T(8,128)S(1)}, f32[8,128]{1,0:T(8,128)S(1)}) custom-call(s32[1,4]{1,0:T(1,128)} %lens_in.1, bf16[128,768]{1,0:T(8,128)(2,1)} %bitcast.6, bf16[768,128]{1,0:T(8,128)(2,1)} %proj_in.1, bf16[4,512,768]{2,1,0:T(8,128)(2,1)} %bitcast.5), custom_call_target="tpu_custom_call" | custom-call | tf_op jit(solution)/shard_map/pallas_call | solution.py:392
  27.7 1.6 %shard_map.76 = (f32[128,128]{1,0:T(8,128)}, f32[4,512,128]{2,1,0:T(8,128)}, f32[768,128]{1,0:T(8,128)}, f32[1,1]{1,0:T(1,128)}) custom-call(f32[128,128]{1,0:T(8,128)S(1)} %get-tuple-element.12.qg, f32[4,512,128]{2,1,0:T(8,128)S(1)} %get-tuple-element.13.pg, f32[768,128]{1,0:T(8,128)S(1)} %get-tuple-element.14.wg, f32[8,128]{1,0:T(8,128)S(1)} %get-tuple-element.15.loss), custom_call_target="tpu_custom_call" | custom-call | tf_op jit(solution)/shard_map/pallas_call | solution.py:442

commit v5 on v4

--- a/solution.py
+++ b/solution.py
@@ -143,7 +143,7 @@
     pairs = [(qhid_in, hid.at[pl.ds(ntp, ntok)]), (proj_in, proj), (lens_in, lens)]
     pairs += [(phid.at[p], hid.at[pl.ds(p * plen, plen)]) for p in range(npass)]
     for n, (src, dst) in enumerate(pairs):
-        load = pltpu.make_async_copy(src, dst, in_sem.at[n])
+        load = pltpu.make_async_copy(src, dst, in_sem.at[min(n, 3)])
         load.start()
         loads.append(load)
     ppad, qpad = sc.shape[1:]
@@ -160,7 +160,7 @@
     loads[1].wait()
     tok[0] = jnp.dot(hid[ntp : ntp + ntok, :], proj[...], preferred_element_type=F32).astype(BF16)
     pl.semaphore_wait(barrier, greeted)
-    tok_copies = [start_copy(tok.at[0], tok.at[k], tok_s.at[k - 1], tok_r.at[k - 1], blk_peer(k)) for k in range(nblk - 1, 0, -1)][::-1]
+    tok_copies = [start_copy(tok.at[0], tok.at[k], tok_s.at[0], tok_r.at[k - 1], blk_peer(k)) for k in range(nblk - 1, 0, -1)][::-1]
     relayed = paired and nblk == 4
     half = ntok // 2
 
@@ -177,6 +177,9 @@
 
     def relay(h):
         if relayed:
+            if h >= 2:
+                for k in (1, 2):
+                    send_hid(h, k, k, 0, (k + 2) % 2 * half, half, parts + h)
             hid_bytes(h, 2 * half, h).wait_recv()
             send_hid(h, 2, 3, 1, 0, half, parts + h)
             send_hid(h, 1, 3, 2, half, half, parts + h)
@@ -185,7 +188,8 @@
         for turn in range(2):
             for h in range(parts):
                 for k in (1, 2):
-                    send_hid(h, k, k, 0, (k + 1 + turn) % 2 * half, half, turn * parts + h)
+                    if turn == 0 or h < 2:
+                        send_hid(h, k, k, 0, (k + 1 + turn) % 2 * half, half, turn * parts + h)
         late_rows, sent_rows = 4 * half, 6 * half
     else:
         for h in range(parts):
@@ -196,9 +200,9 @@
         tell(1)
 
     loads[2].wait()
+    pltpu.make_async_copy(hid.at[pl.ds(0, ntp)], hid.at[pl.ds(0, ntp)], in_sem.at[3]).wait()
     size = jnp.ones((ppad, LANES), jnp.int32)
     for p in range(npass):
-        loads[3 + p].wait()
         vec = jnp.dot(hid[p * plen : (p + 1) * plen, :], proj[...], preferred_element_type=F32).astype(BF16)
         ptok[p, :, :dim] = vec
         out_of = (rows_iota((plen, LANES), 0) >= lens[0, p]) & (rows_iota((plen, LANES), 1) == 0)
@@ -334,9 +338,8 @@
             bytes_of(zbuf.at[h, pl.ds(0, nz - 1)], z_s.at[0], z_r.at[h]).wait_recv()
         cbuf[h, me_a] = jnp.sum(zbuf[h].astype(F32), 0).astype(BF16)
         share(lambda k: cbuf.at[h, me_a], lambda k: cbuf.at[h, me_a], c_s.at[0], c_r.at[h], a_peer, na)
-    for copy in tok_copies:
-        copy.wait_send()
     if nblk > 1:
+        bytes_of(tok.at[pl.ds(1, nblk - 1)], tok_s.at[0], tok_r.at[0]).wait_send()
         bytes_of(hid.at[pl.ds(ntp, sent_rows)], hid_s.at[0], hid_r.at[0]).wait_send()
         sc_all.wait_send()
         qg_all.wait_send()
@@ -355,13 +358,13 @@
         bytes_of(cbuf.at[:, pl.ds(0, na - 1)], c_s.at[0], c_r.at[0]).wait_send()
 
 
-def write_out(qg, pg, wg, loss, qg_out, pg_out, wg_out, loss_out, sem):
+def write_out(qg, pg, wg, loss, qg_out, pg_out, wg_out, loss_out, held, sem):
+    held[0, 0] = loss[0, 0]
     copies = []
-    for n, (src, dst) in enumerate(((pg, pg_out), (wg, wg_out), (qg, qg_out))):
+    for n, (src, dst) in enumerate(((pg, pg_out), (wg, wg_out), (qg, qg_out), (held, loss_out))):
         copy = pltpu.make_async_copy(src, dst, sem.at[n])
         copy.start()
         copies.append(copy)
-    loss_out[0, 0] = loss[0, 0]
     for copy in copies:
         copy.wait()
 
@@ -386,7 +389,7 @@
     vmem = pl.BlockSpec(memory_space=pltpu.VMEM)
     sem = lambda *n: pltpu.SemaphoreType.DMA(tuple(max(i, 1) for i in n))
     flag = pltpu.SemaphoreType.REGULAR((max(nz - 2, 1),))
-    pairs = [sem(nblk - 1), sem(nblk - 1), sem(1), sem(2 * parts)]
+    pairs = [sem(1), sem(nblk - 1), sem(1), sem(2 * parts)]
     pairs += [sem(1)] * 8
     pairs += [sem(1), sem(parts)] * 3
     held = pl.pallas_call(
@@ -425,7 +428,7 @@
             pltpu.VMEM((parts, na, deep, dim), BF16),
             pltpu.VMEM((parts, nz, deep, dim), BF16),
             pltpu.VMEM((parts, na, deep, dim), BF16),
-            sem(npass + 3),
+            sem(4),
             flag,
             flag,
         ] + pairs,
@@ -448,8 +451,8 @@
             jax.ShapeDtypeStruct((1, 1), F32),
         ),
         in_specs=[vmem] * 4,
-        out_specs=(hbm, hbm, hbm, pl.BlockSpec(memory_space=pltpu.SMEM)),
-        scratch_shapes=[sem(3)],
+        out_specs=(hbm, hbm, hbm, hbm),
+        scratch_shapes=[pltpu.SMEM((1, 1), F32), sem(4)],
         compiler_params=pltpu.CompilerParams(vmem_limit_bytes=8 << 20),
     )(*[pltpu.with_memory_space_constraint(x, pltpu.VMEM) for x in held])
     return (

time: 29.5 us -> 28.8 us (0.976)
  Pallas kernels: 28.7 us -> 28 us
    pallas_call x1, Pallas kernels: 1.65 us -> 1.15 us  [shards(): pl.pallas_call(write_out, out_shape=(jax.ShapeDtypeStruct((ntok, dim), F3...]
where the time goes in v5:
time: 28.8 us; the launch traced here: 28.6 us
  Pallas kernels  28 us (97%)
  between operations  0.64 us (2%)
    pallas_call x1, Pallas kernels, shards(): pl.pallas_call(functools.partial(kernel, dims), out_shape=(pltpu.VMEM((nt...  26.8 us
    pallas_call x1, Pallas kernels, shards(): pl.pallas_call(write_out, out_shape=(jax.ShapeDtypeStruct((ntok, dim), F3...  1.15 us

profile of v5, /device:TPU:0, one launch (start us, length us, event | category | flops | bytes accessed | tf_op | source)
XLA Modules:
  0.0 28.6 jit_solution(911877283512829756)
XLA Ops:
  0.6 26.8 %shard_map.75 = (f32[128,128]{1,0:T(8,128)S(1)}, f32[4,512,128]{2,1,0:T(8,128)S(1)}, f32[768,128]{1,0:T(8,128)S(1)}, f32[8,128]{1,0:T(8,128)S(1)}) custom-call(s32[1,4]{1,0:T(1,128)} %lens_in.1, bf16[128,768]{1,0:T(8,128)(2,1)} %bitcast.6, bf16[768,128]{1,0:T(8,128)(2,1)} %proj_in.1, bf16[4,512,768]{2,1,0:T(8,128)(2,1)} %bitcast.5), custom_call_target="tpu_custom_call" | custom-call | tf_op jit(solution)/shard_map/pallas_call | solution.py:395
  27.5 1.2 %shard_map.76 = (f32[128,128]{1,0:T(8,128)}, f32[4,512,128]{2,1,0:T(8,128)}, f32[768,128]{1,0:T(8,128)}, f32[1,1]{1,0:T(1,128)}) custom-call(f32[128,128]{1,0:T(8,128)S(1)} %get-tuple-element.12.qg, f32[4,512,128]{2,1,0:T(8,128)S(1)} %get-tuple-element.13.pg, f32[768,128]{1,0:T(8,128)S(1)} %get-tuple-element.14.wg, f32[8,128]{1,0:T(8,128)S(1)} %get-tuple-element.15.loss), custom_call_target="tpu_custom_call" | custom-call | tf_op jit(solution)/shard_map/pallas_call | solution.py:445

commit v6 on v5

--- a/solution.py
+++ b/solution.py
@@ -185,11 +185,6 @@
             send_hid(h, 1, 3, 2, half, half, parts + h)
 
     if relayed:
-        for turn in range(2):
-            for h in range(parts):
-                for k in (1, 2):
-                    if turn == 0 or h < 2:
-                        send_hid(h, k, k, 0, (k + 1 + turn) % 2 * half, half, turn * parts + h)
         late_rows, sent_rows = 4 * half, 6 * half
     else:
         for h in range(parts):
@@ -209,6 +204,12 @@
         ptok[p, :, dim:] = jnp.where(out_of, FAR, 0.0).astype(BF16)
         ptok_t[p] = vec.T
         size = jnp.where(rows_iota((ppad, LANES), 0) == p, lens[0, p], size)
+        if relayed and p == 0:
+            for turn in range(2):
+                for h in range(parts):
+                    for k in (1, 2):
+                        if turn == 0 or h < 2:
+                            send_hid(h, k, k, 0, (k + 1 + turn) % 2 * half, half, turn * parts + h)
 
     def forward(first, count):
         width = count * ntok
@@ -359,9 +360,10 @@
 
 
 def write_out(qg, pg, wg, loss, qg_out, pg_out, wg_out, loss_out, held, sem):
-    held[0, 0] = loss[0, 0]
     copies = []
     for n, (src, dst) in enumerate(((pg, pg_out), (wg, wg_out), (qg, qg_out), (held, loss_out))):
+        if n == 3:
+            held[0, 0] = loss[0, 0]
         copy = pltpu.make_async_copy(src, dst, sem.at[n])
         copy.start()
         copies.append(copy)

time: 28.8 us -> 28.8 us (level)
  no operation moved by 1% of the time
where the time goes in v6:
time: 28.8 us; the launch traced here: 28.6 us
  Pallas kernels  28 us (97%)
  between operations  0.64 us (2%)
    pallas_call x1, Pallas kernels, shards(): pl.pallas_call(functools.partial(kernel, dims), out_shape=(pltpu.VMEM((nt...  26.8 us
    pallas_call x1, Pallas kernels, shards(): pl.pallas_call(write_out, out_shape=(jax.ShapeDtypeStruct((ntok, dim), F3...  1.15 us

profile of v6, /device:TPU:0, one launch (start us, length us, event | category | flops | bytes accessed | tf_op | source)
XLA Modules:
  0.0 28.6 jit_solution(5234042991853209392)
XLA Ops:
  0.6 26.8 %shard_map.75 = (f32[128,128]{1,0:T(8,128)S(1)}, f32[4,512,128]{2,1,0:T(8,128)S(1)}, f32[768,128]{1,0:T(8,128)S(1)}, f32[8,128]{1,0:T(8,128)S(1)}) custom-call(s32[1,4]{1,0:T(1,128)} %lens_in.1, bf16[128,768]{1,0:T(8,128)(2,1)} %bitcast.6, bf16[768,128]{1,0:T(8,128)(2,1)} %proj_in.1, bf16[4,512,768]{2,1,0:T(8,128)(2,1)} %bitcast.5), custom_call_target="tpu_custom_call" | custom-call | tf_op jit(solution)/shard_map/pallas_call | solution.py:397
  27.5 1.2 %shard_map.76 = (f32[128,128]{1,0:T(8,128)}, f32[4,512,128]{2,1,0:T(8,128)}, f32[768,128]{1,0:T(8,128)}, f32[1,1]{1,0:T(1,128)}) custom-call(f32[128,128]{1,0:T(8,128)S(1)} %get-tuple-element.12.qg, f32[4,512,128]{2,1,0:T(8,128)S(1)} %get-tuple-element.13.pg, f32[768,128]{1,0:T(8,128)S(1)} %get-tuple-element.14.wg, f32[8,128]{1,0:T(8,128)S(1)} %get-tuple-element.15.loss), custom_call_target="tpu_custom_call" | custom-call | tf_op jit(solution)/shard_map/pallas_call | solution.py:447
